TPU v7x, 32 devices: a whole 2x2x4 slice. The times are simulated.
32 devices in a mesh: les: 8 (over y, x, core), modes: 4 (over z).
Axes of the slice: x: 2, y: 2, z: 4, core: 2. Of those that a mesh axis runs over, the one named last changes fastest.
Arguments:
- pressure: bfloat16 [65536, 512], P('les', 'modes'), may hold values from -6 to 6
- targets: int32 [65536], P('les'), may hold values from 0 to 32767, as said below
- counts: int32 [8], P('les'), may hold values from 1 to 8192, as said below
- pseudo_inverse: bfloat16 [2, 1536, 16384], P(None, None, ('les', 'modes')), may hold values from -0.046875 to 0.046875
Outputs:
- harmonics: float32 [2, 2, 8, 1536], P(None, None, None, ('les', 'modes'))
Inputs may be any that keep to these rules, and one draw needn't show every extreme that they name: `counts`: some partition holds exactly 8192 live faces; all partitions together hold 32768. `targets`: the live slots (slot f of partition i with f < counts[i]) name every station point exactly once. Point p of a station lies in the point rows of les index p // (512 * 4); at most 1024 live faces of one partition lie in the point rows of one les index, and some partition reaches that bound. Slots that are not live hold arbitrary indices in the range.
All inputs are finite; a program needn't handle non-finite values.
Results may differ from a plain program's by a relative error of at most 0.0003.
Values may be sent and summed in bfloat16 or wider, within the bound.
A program may use at most 64 MiB of HBM per device.

v0:
```python
import math
import jax
import jax.numpy as jnp
from jax import lax
from jax.sharding import PartitionSpec as P

TIME = 512
HARM = 8


def fourier_rows():
    sample_ids = jnp.arange(TIME, dtype=jnp.int32)
    orders = jnp.arange(1, HARM + 1, dtype=jnp.int32)
    phase_ids = orders[:, None] * sample_ids[None, :] % TIME
    angles = phase_ids.astype(jnp.float32) * (2.0 * math.pi / TIME)
    scale_factor = math.sqrt(2.0 / TIME)
    return jnp.stack([jnp.cos(angles), -jnp.sin(angles)]) * scale_factor


def rank_by_owner(dest_les, is_live, les_count):
    face_slots = dest_les.shape[0]
    span_width = math.gcd(face_slots, 128)
    owner_ids = jnp.arange(les_count, dtype=jnp.int32)
    matches = ((dest_les[None, :] == owner_ids[:, None]) & is_live[None, :]).astype(jnp.float32)
    matches = matches.reshape(les_count, face_slots // span_width, span_width)
    position = jnp.arange(span_width, dtype=jnp.int32)
    upper = (position[:, None] <= position[None, :]).astype(jnp.float32)
    within = jnp.einsum("nbj,jw->nbw", matches, upper, precision=lax.Precision.HIGHEST)
    block_sums = jnp.sum(matches, axis=2)
    before = jnp.cumsum(block_sums, axis=1) - block_sums
    running = within + before[:, :, None]
    ranked = jnp.sum(running * matches, axis=0).reshape(face_slots) - 1.0
    return ranked.astype(jnp.int32)


def local(pressure, targets, counts, pseudo_inverse):
    les_count = lax.axis_size("les")
    mode_count = lax.axis_size("modes")
    block_len = pressure.shape[1]
    face_slots = targets.shape[0]
    stations = pseudo_inverse.shape[0]
    mode_total = pseudo_inverse.shape[1]
    point_dev = pseudo_inverse.shape[2]
    rows_les = point_dev * mode_count
    points_all = rows_les * les_count
    send_cap = face_slots // les_count
    send_total = les_count * send_cap
    slot_ids = jnp.arange(face_slots, dtype=jnp.int32)
    is_live = slot_ids < counts[0]
    station_of = targets // points_all
    point_of = targets % points_all
    dest_les = point_of // rows_les
    local_row = station_of * rows_les + point_of % rows_les
    face_rank = rank_by_owner(dest_les, is_live, les_count)
    send_pos = jnp.where(is_live, dest_les * send_cap + face_rank, send_total)
    source_face = jnp.full((send_total,), -1, jnp.int32).at[send_pos].set(slot_ids, mode="drop")
    slot_used = source_face >= 0
    source_safe = jnp.maximum(source_face, 0)
    row_tags = jnp.where(slot_used, jnp.take(local_row, source_safe, axis=0), -1).reshape(
        1, send_total
    )
    tags_in = lax.all_to_all(row_tags, "les", split_axis=1, concat_axis=1, tiled=True)
    arrival = jnp.where(tags_in[0] >= 0, tags_in[0], stations * rows_les)
    arrival_ids = jnp.arange(send_total, dtype=jnp.int32)
    arrived_from = (
        jnp.zeros((stations * rows_les,), jnp.int32).at[arrival].set(arrival_ids, mode="drop")
    )
    fourier = fourier_rows()
    block_start = lax.axis_index("modes") * block_len
    block_rows = lax.dynamic_slice_in_dim(fourier, block_start, block_len, 2)
    block_rows = block_rows.reshape(2 * HARM, block_len)
    spectra = lax.dot_general(
        pressure.astype(jnp.float32),
        block_rows,
        (((1,), (1,)), ((), ())),
        precision=lax.Precision.HIGHEST,
    )
    picked = jnp.take(spectra, source_safe, axis=0)
    outgoing = jnp.where(slot_used[:, None], picked, jnp.zeros_like(picked))
    incoming = lax.all_to_all(outgoing, "les", split_axis=0, concat_axis=0, tiled=True)
    gathered = jnp.take(incoming, arrived_from, axis=0)
    gathered = gathered.reshape(stations, rows_les, 2 * HARM)
    summed = lax.psum_scatter(gathered, "modes", scatter_dimension=1, tiled=True)
    partial_value = []
    for station_index in range(stations):
        weights = pseudo_inverse[station_index].astype(jnp.float32)
        projected = lax.dot_general(
            summed[station_index],
            weights,
            (((0,), (1,)), ((), ())),
            precision=lax.Precision.HIGHEST,
        )
        partial_value.append(projected.reshape(2, HARM, mode_total))
    shares = jnp.stack(partial_value)
    return lax.psum_scatter(shares, ("les", "modes"), scatter_dimension=3, tiled=True)


def solution(mesh):
    placed = (P("les", "modes"), P("les"), P("les"), P(None, None, ("les", "modes")))
    return jax.shard_map(
        local,
        mesh=mesh,
        in_specs=placed,
        out_specs=P(None, None, None, ("les", "modes")),
        check_vma=False,
    )
```

profile of v0, /device:TPU:0, one launch (start us, length us, event | category | flops | bytes accessed | tf_op | source)
XLA Modules:
  0.0 323.5 jit_solution(5124301517689672651)
XLA Ops:
  7.4 0.8 fusion.13
  8.2 0.1 convert_reduce_fusion
  8.3 0.2 reduce_window_sum.11
  8.6 0.2 fusion.5
  8.8 0.8 compare_select_fusion.2
  9.6 30.5 %scatter_custom_fusion = s32[8192]{0:T(1024)S(1)} fusion(s32[8192]{0:T(1024)S(1)} %compare_select_fusion.2, s32[8192]{0:T(1024)S(1)} %iota.64, s32[]{:T(128)} %constant.117.clone.1), kind=kCustom, calls=%fused_computation.68 | custom fusion | bytes 32772 | tf_op jit(solution)/shard_map/scatter | solution.py:56
  40.1 45.5 %gather_fusion = s32[8192]{0:T(1024)S(1)} fusion(s32[8192]{0:T(1024)S(1)} %get-tuple-element.8, s32[8192]{0:T(1024)S(1)} %maximum_clamp_fusion), kind=kCustom, calls=%fused_computation | custom fusion | bytes 98304 | tf_op jit(solution)/shard_map/jit(_take)/gather | solution.py:59
  85.6 0.6 select_select_fusion.1
  86.3 5.2 %all-to-all-start = ((s32[1,8,1024]{2,0,1:T(1,128)}), s32[1,8,1024]{2,0,1:T(1,128)S(1)}, u32[]{:S(2)}, u32[]{:S(2)}) async-start(s32[1,8,1024]{2,0,1:T(1,128)} %bitcast.4), calls=%async_computation | async-start | bytes 65536 | tf_op jit(solution)/shard_map/all_to_all | solution.py:62
  91.4 0.2 sine_negate_fusion
  91.7 1.7 convolution_bitcast_fusion
  93.4 2.6 copy.9
  96.0 29.9 %gather_fusion.1 = f32[8192,16]{1,0:T(8,128)} fusion(f32[8192,16]{1,0:T(8,128)} %copy.9, s32[8192]{0:T(1024)S(1)} %maximum_clamp_fusion), kind=kCustom, calls=%fused_computation.1 | custom fusion | bytes 1081344 | tf_op jit(solution)/shard_map/jit(_take)/gather | solution.py:78
  125.9 2.8 copy.10
  128.7 0.9 select_select_fusion
  129.6 4.2 %all-to-all-start.1 = ((f32[8,1024,16]{1,2,0:T(8,128)}), f32[8,1024,16]{1,2,0:T(8,128)S(1)}, u32[]{:S(2)}, u32[]{:S(2)}) async-start(f32[8,1024,16]{1,2,0:T(8,128)} %select_select_fusion), calls=%async_computation.1 | async-start | bytes 1048576 | tf_op jit(solution)/shard_map/all_to_all | solution.py:80
  133.8 0.0 reduce-scatter.5.cloned.1.call-start
  133.8 0.1 compare_select_fusion
  133.9 30.5 %scatter_custom_fusion.1 = s32[4096]{0:T(1024)S(1)} fusion(s32[8192]{0:T(1024)S(1)} %bitcast.62, s32[8192]{0:T(1024)S(1)} %iota.65, s32[]{:T(128)} %constant.116.clone.1), kind=kCustom, calls=%fused_computation.77 | custom fusion | bytes 16388 | tf_op jit(solution)/shard_map/scatter | solution.py:66
  164.4 2.6 copy.11
  167.0 16.3 %gather_fusion.2 = f32[4096,16]{1,0:T(8,128)} fusion(f32[8192,16]{1,0:T(8,128)} %bitcast.56, s32[4096]{0:T(1024)S(1)} %fusion.27), kind=kCustom, calls=%fused_computation.2 | custom fusion | bytes 540672 | tf_op jit(solution)/shard_map/jit(_take)/gather | solution.py:81
  183.3 2.2 copy.12
  185.4 0.7 broadcast_select_fusion
  186.2 0.0 reduce-scatter.7.cloned.1.call-start
  186.2 21.4 %reduce-scatter.5.cloned.1.call-done = f32[2,512,16]{1,2,0:T(8,128)} async-done(((f32[2,2048,16]{1,2,0:T(8,128)}), f32[2,512,16]{1,2,0:T(8,128)}) %reduce-scatter.5.cloned.1.call-update) | async-done | bytes 65552 | tf_op jit(solution)/shard_map/reduce_scatter | solution.py:83
  207.7 2.7 convolution_bitcast_fusion.1
  210.4 2.8 convolution_bitcast_fusion.2
  213.2 3.3 %copy.13 = f32[2,2,8,1536]{2,1,0,3:T(2,128)} copy(f32[2,2,8,1536]{3,2,1,0:T(8,128)S(1)} %pad_maximum_fusion) | data formatting | bytes 393216
  216.5 4.7 %reshape.276 = f32[1536,32]{1,0:T(8,128)} reshape(f32[1536,2,2,8]{3,2,1,0:T(2,128)} %bitcast.58) | data formatting | bytes 393216
  221.2 93.9 %reduce-scatter.7.cloned.1.call-done = f32[48,32]{1,0:T(8,128)} async-done(((f32[1536,32]{1,0:T(8,128)}), f32[48,32]{1,0:T(8,128)}) %reduce-scatter.7.cloned.1.call-update) | async-done | bytes 6160
  315.1 0.9 reshape.277
  315.9 0.7 copy.14
  (18 shorter events, 0.2 us)
Async XLA Ops:
  6.5 85.1 %copy-start = (bf16[8192,128]{1,0:T(8,128)(2,1)S(1)}, bf16[8192,128]{1,0:T(8,128)(2,1)}, u32[]{:S(2)}) copy-start(bf16[8192,128]{1,0:T(8,128)(2,1)} %param.4) | copy-start | bytes 6291460
  86.3 43.3 %all-to-all-start = ((s32[1,8,1024]{2,0,1:T(1,128)}), s32[1,8,1024]{2,0,1:T(1,128)S(1)}, u32[]{:S(2)}, u32[]{:S(2)}) async-start(s32[1,8,1024]{2,0,1:T(1,128)} %bitcast.4), calls=%async_computation | async-start | bytes 65536 | tf_op jit(solution)/shard_map/all_to_all | solution.py:62
  129.6 34.8 %all-to-all-start.1 = ((f32[8,1024,16]{1,2,0:T(8,128)}), f32[8,1024,16]{1,2,0:T(8,128)S(1)}, u32[]{:S(2)}, u32[]{:S(2)}) async-start(f32[8,1024,16]{1,2,0:T(8,128)} %select_select_fusion), calls=%async_computation.1 | async-start | bytes 1048576 | tf_op jit(solution)/shard_map/all_to_all | solution.py:80
  133.8 73.9 %reduce-scatter.5.cloned.1.call-start = ((), (), s32[]{:S(2)}) async-start(), calls=%async_computation.4 | async-start | bytes 327680 | tf_op jit(solution)/shard_map/reduce_scatter | solution.py:83
  186.2 128.9 %reduce-scatter.7.cloned.1.call-start = ((), (), s32[]{:S(2)}) async-start(), calls=%async_computation.5 | async-start | bytes 811008
Sparse Core Ops, SparseCore 0:
  186.3 21.3 reduce-scatter.4
  221.3 93.6 reduce-scatter.6
where the time goes:
time: 324 us; the launch traced here: 323 us
  local copies, waits for them, and re-layouts  172 us (53%)
  waiting for transfers between devices  115 us (35%)
  between operations  14.4 us (4%)
  starting transfers between devices  9.44 us (3%)
  matrix products  7.45 us (2%)
  other arithmetic  4.52 us (1%)
    unnamed x3, waiting for transfers between devices  93.9 us
    gather x1, local copies, waits for them, and re-layouts, local(): jnp.take(local_row, source_safe, axis=0)  45.5 us
    gather x2, local copies, waits for them, and re-layouts, local(): picked = jnp.take(spectra, source_safe, axis=0)  32.7 us
    scatter x1, local copies, waits for them, and re-layouts, local(): jnp.full((send_total,), -1, jnp.int32).at[send_pos]  30.5 us
    scatter x1, local copies, waits for them, and re-layouts, local(): jnp.zeros((stations * rows_les,), jnp.int32).at[arrival]  30.5 us
    reduce_scatter x1, waiting for transfers between devices, local(): lax.psum_scatter(gathered, 'modes', scatter_dimension=1, tiled=True)  21.4 us
    gather x2, local copies, waits for them, and re-layouts, local(): gathered = jnp.take(incoming, arrived_from, axis=0)  18.4 us
    unnamed x6, local copies, waits for them, and re-layouts  9.54 us
  transfers between devices with their start and end apart: 4, of which 2 were waited for; matrix products, arithmetic and copies ran while one was open for 21% of the time, Pallas kernels for 0%

commit v1 on v0

--- a/solution.py
+++ b/solution.py
@@ -3,9 +3,24 @@
 import jax.numpy as jnp
 from jax import lax
 from jax.sharding import PartitionSpec as P
+from jax.lax import axis_index, axis_size, ppermute
 
 TIME = 512
 HARM = 8
+
+
+def _convert_desk(field_in, d0, slab_in):
+    vec_out, outcome_arr = (field_in.shape[:d0], field_in.shape[d0 + 1 :])
+    finding = field_in.reshape(*vec_out, slab_in, -1, *outcome_arr)
+    return jnp.moveaxis(finding, d0, 0)
+
+
+def scan_weights_now(my_tile, in_dim):
+    my_tile = jnp.moveaxis(my_tile, 0, in_dim)
+    m_next = my_tile.shape
+    return my_tile.reshape(
+        *m_next[:in_dim], m_next[in_dim] * m_next[in_dim + 1], *m_next[in_dim + 2 :]
+    )
 
 
 def fourier_rows():
@@ -77,7 +92,22 @@
     )
     picked = jnp.take(spectra, source_safe, axis=0)
     outgoing = jnp.where(slot_used[:, None], picked, jnp.zeros_like(picked))
-    incoming = lax.all_to_all(outgoing, "les", split_axis=0, concat_axis=0, tiled=True)
+
+    def connect_cycles(payload, mesh_dim, local_x, matrix):
+        z_new = axis_index(mesh_dim)
+        t_next = axis_size(mesh_dim)
+        e_now, kept_arr = (t_next, z_new)
+        mat_out = _convert_desk(payload, local_x, e_now)
+        vals = [mat_out[kept_arr]]
+        for b in [*range(1, e_now)]:
+            item_now = mat_out[(kept_arr + b) % e_now]
+            shaped = ppermute(item_now, mesh_dim, [(ii, (ii + b) % e_now) for ii in range(e_now)])
+            vals.append(shaped)
+        reached = jnp.stack(vals)
+        mat_out = reached[(kept_arr - jnp.arange(e_now)) % e_now]
+        return scan_weights_now(mat_out, matrix)
+
+    incoming = connect_cycles(outgoing, "les", 0, 0)
     gathered = jnp.take(incoming, arrived_from, axis=0)
     gathered = gathered.reshape(stations, rows_les, 2 * HARM)
     summed = lax.psum_scatter(gathered, "modes", scatter_dimension=1, tiled=True)

time: 324 us -> 333 us (1.028)
  waiting for transfers between devices: 115 us -> 123 us
    ppermute x0 -> x7, waiting for transfers between devices: none -> 9.46 us  [connect_cycles(): ppermute(item_now, mesh_dim, [(ii, (ii + b) % e_now) for ii in range(e_no...]
    ppermute x0 -> x7, starting transfers between devices: none -> 5.96 us  [connect_cycles(): ppermute(item_now, mesh_dim, [(ii, (ii + b) % e_now) for ii in range(e_no...]
    all_to_all x1 -> x0, starting transfers between devices: 4.2 us -> none  [local(): lax.all_to_all(outgoing, 'les', split_axis=0, concat_axis=0, tiled=True)]
    unnamed x6 -> x12, local copies, waits for them, and re-layouts: 9.54 us -> 9.53 us
  transfers between devices with their start and end apart: 4 -> 10, of which waited for: 2 -> 4; matrix products, arithmetic and copies ran while one was open for 21% -> 20% of each run, Pallas kernels for 0% -> 0%
where the time goes in v1:
time: 333 us
  local copies, waits for them, and re-layouts  173 us (52%)
  waiting for transfers between devices  123 us (37%)
  between operations  14.6 us (4%)
  starting transfers between devices  11.2 us (3%)
  matrix products  7.45 us (2%)
  other arithmetic  3.75 us (1%)
    unnamed x3, waiting for transfers between devices  94 us
    gather x1, local copies, waits for them, and re-layouts, local(): jnp.take(local_row, source_safe, axis=0)  45.5 us
    gather x2, local copies, waits for them, and re-layouts, local(): picked = jnp.take(spectra, source_safe, axis=0)  32.7 us
    scatter x1, local copies, waits for them, and re-layouts, local(): jnp.full((send_total,), -1, jnp.int32).at[send_pos]  30.5 us
    scatter x1, local copies, waits for them, and re-layouts, local(): jnp.zeros((stations * rows_les,), jnp.int32).at[arrival]  30.5 us
    reduce_scatter x1, waiting for transfers between devices, local(): lax.psum_scatter(gathered, 'modes', scatter_dimension=1, tiled=True)  19.1 us
    gather x2, local copies, waits for them, and re-layouts, local(): gathered = jnp.take(incoming, arrived_from, axis=0)  18.4 us
    unnamed x12, local copies, waits for them, and re-layouts  9.53 us
  transfers between devices with their start and end apart: 10, of which 4 were waited for; matrix products, arithmetic and copies ran while one was open for 20% of the time, Pallas kernels for 0%

profile of v1, /device:TPU:0, one launch (start us, length us, event | category | flops | bytes accessed | tf_op | source)
XLA Modules:
  0.0 332.7 jit_solution(18415730966426722504)
XLA Ops:
  7.4 0.8 fusion.13
  8.3 0.2 reduce_window_sum.11
  8.6 0.2 fusion.5
  8.8 0.8 compare_select_fusion.2
  9.6 30.5 %scatter_custom_fusion = s32[8192]{0:T(1024)S(1)} fusion(s32[8192]{0:T(1024)S(1)} %compare_select_fusion.2, s32[8192]{0:T(1024)S(1)} %iota.68, s32[]{:T(128)} %constant.171.clone.1), kind=kCustom, calls=%fused_computation.84 | custom fusion | bytes 32772 | tf_op jit(solution)/shard_map/scatter | solution.py:71
  40.1 45.5 %gather_fusion = s32[8192]{0:T(1024)S(1)} fusion(s32[8192]{0:T(1024)S(1)} %get-tuple-element.16, s32[8192]{0:T(1024)S(1)} %maximum_clamp_fusion), kind=kCustom, calls=%fused_computation | custom fusion | bytes 98304 | tf_op jit(solution)/shard_map/jit(_take)/gather | solution.py:74
  85.6 0.6 select_select_fusion.1
  86.3 5.2 %all-to-all-start = ((s32[1,8,1024]{2,0,1:T(1,128)}), s32[1,8,1024]{2,0,1:T(1,128)S(1)}, u32[]{:S(2)}, u32[]{:S(2)}) async-start(s32[1,8,1024]{2,0,1:T(1,128)} %bitcast.4), calls=%async_computation | async-start | bytes 65536 | tf_op jit(solution)/shard_map/all_to_all | solution.py:77
  91.8 1.7 convolution_bitcast_fusion
  93.6 2.6 copy.9
  96.2 29.9 %gather_fusion.1 = f32[8192,16]{1,0:T(8,128)} fusion(f32[8192,16]{1,0:T(8,128)} %copy.9, s32[8192]{0:T(1024)S(1)} %maximum_clamp_fusion), kind=kCustom, calls=%fused_computation.1 | custom fusion | bytes 1081344 | tf_op jit(solution)/shard_map/jit(_take)/gather | solution.py:93
  126.1 2.8 copy.10
  129.1 2.6 collective-permute-start.6
  131.7 0.6 collective-permute-start.5
  132.3 1.4 collective-permute-start.3
  133.8 1.2 collective-permute-start
  135.1 30.5 %scatter_custom_fusion.1 = s32[4096]{0:T(1024)S(1)} fusion(s32[8192]{0:T(1024)S(1)} %bitcast.92, s32[8192]{0:T(1024)S(1)} %iota.69, s32[]{:T(128)} %constant.170.clone.1), kind=kCustom, calls=%fused_computation.93 | custom fusion | bytes 16388 | tf_op jit(solution)/shard_map/scatter | solution.py:81
  165.7 5.1 %collective-permute-done.1 = f32[1024,16]{0,1:T(8,128)S(1)} collective-permute-done((f32[1024,16]{0,1:T(8,128)S(1)}, f32[1024,16]{0,1:T(8,128)S(1)}, u32[]{:S(2)}, u32[]{:S(2)}) %collective-permute-start.1) | collective-permute-done | bytes 65568 | tf_op jit(solution)/shard_map/ppermute | solution.py:104
  170.8 4.3 %collective-permute-done.2 = f32[1024,16]{0,1:T(8,128)S(1)} collective-permute-done((f32[1024,16]{0,1:T(8,128)S(1)}, f32[1024,16]{0,1:T(8,128)S(1)}, u32[]{:S(2)}, u32[]{:S(2)}) %collective-permute-start.2) | collective-permute-done | bytes 65568 | tf_op jit(solution)/shard_map/ppermute | solution.py:104
  175.3 0.6 gather_fusion.2
  175.8 2.6 copy.11
  178.5 16.3 %gather_fusion.3 = f32[4096,16]{1,0:T(8,128)} fusion(f32[8192,16]{1,0:T(8,128)} %bitcast.86, s32[4096]{0:T(1024)S(1)} %fusion.27), kind=kCustom, calls=%fused_computation.3 | custom fusion | bytes 540672 | tf_op jit(solution)/shard_map/jit(_take)/gather | solution.py:111
  194.7 2.2 copy.12
  196.9 0.7 broadcast_select_fusion
  197.7 19.1 %reduce-scatter.5.cloned.1.call-done = f32[2,512,16]{1,2,0:T(8,128)} async-done(((f32[2,2048,16]{1,2,0:T(8,128)}), f32[2,512,16]{1,2,0:T(8,128)}) %reduce-scatter.5.cloned.1.call-update) | async-done | bytes 65552 | tf_op jit(solution)/shard_map/reduce_scatter | solution.py:113
  216.8 2.7 convolution_bitcast_fusion.1
  219.6 2.8 convolution_bitcast_fusion.2
  222.4 3.3 copy.13
  225.6 4.7 %reshape.336 = f32[1536,32]{1,0:T(8,128)} reshape(f32[1536,2,2,8]{3,2,1,0:T(2,128)} %bitcast.88) | data formatting | bytes 393216
  230.3 94.0 %reduce-scatter.7.cloned.1.call-done = f32[48,32]{1,0:T(8,128)} async-done(((f32[1536,32]{1,0:T(8,128)}), f32[48,32]{1,0:T(8,128)}) %reduce-scatter.7.cloned.1.call-update) | async-done | bytes 6160
  324.3 0.9 reshape.337
  325.2 0.7 copy.14
  (41 shorter events, 1.0 us)
Async XLA Ops:
  6.5 85.3 %copy-start = (bf16[8192,128]{1,0:T(8,128)(2,1)S(1)}, bf16[8192,128]{1,0:T(8,128)(2,1)}, u32[]{:S(2)}) copy-start(bf16[8192,128]{1,0:T(8,128)(2,1)} %param.4) | copy-start | bytes 6291460
  86.3 48.7 %all-to-all-start = ((s32[1,8,1024]{2,0,1:T(1,128)}), s32[1,8,1024]{2,0,1:T(1,128)S(1)}, u32[]{:S(2)}, u32[]{:S(2)}) async-start(s32[1,8,1024]{2,0,1:T(1,128)} %bitcast.4), calls=%async_computation | async-start | bytes 65536 | tf_op jit(solution)/shard_map/all_to_all | solution.py:77
  91.4 125.4 %reduce-scatter.5.cloned.1.call-start = ((), (), s32[]{:S(2)}) async-start(), calls=%async_computation.3 | async-start | bytes 327680 | tf_op jit(solution)/shard_map/reduce_scatter | solution.py:113
  129.1 46.2 %collective-permute-start.6 = (f32[1024,16]{0,1:T(8,128)S(1)}, f32[1024,16]{0,1:T(8,128)S(1)}, u32[]{:S(2)}, u32[]{:S(2)}) collective-permute-start(f32[1024,16]{0,1:T(8,128)S(1)} %get-tuple-element.8), channel_id=1, source_target_pairs={{0,28},{4,0},{8,4},{12,8},{16,12},{20,16},{24,20},{28,24},{1,29},{... | collective-permute-start | bytes 196616 | tf_op jit(solution)/shard_map/ppermute | solution.py:104
  131.7 43.6 %collective-permute-start.5 = (f32[1024,16]{0,1:T(8,128)S(1)}, f32[1024,16]{0,1:T(8,128)S(1)}, u32[]{:S(2)}, u32[]{:S(2)}) collective-permute-start(f32[1024,16]{0,1:T(8,128)S(1)} %get-tuple-element.9), channel_id=1, source_target_pairs={{0,24},{4,28},{8,0},{12,4},{16,8},{20,12},{24,16},{28,20},{1,25},{... | collective-permute-start | bytes 196616 | tf_op jit(solution)/shard_map/ppermute | solution.py:104
  132.2 43.0 %collective-permute-start.4 = (f32[1024,16]{0,1:T(8,128)S(1)}, f32[1024,16]{0,1:T(8,128)S(1)}, u32[]{:S(2)}, u32[]{:S(2)}) collective-permute-start(f32[1024,16]{0,1:T(8,128)S(1)} %get-tuple-element.10), channel_id=1, source_target_pairs={{0,20},{4,24},{8,28},{12,0},{16,4},{20,8},{24,12},{28,16},{1,21},{... | collective-permute-start | bytes 196616 | tf_op jit(solution)/shard_map/ppermute | solution.py:104
  132.3 42.8 %collective-permute-start.3 = (f32[1024,16]{0,1:T(8,128)S(1)}, f32[1024,16]{0,1:T(8,128)S(1)}, u32[]{:S(2)}, u32[]{:S(2)}) collective-permute-start(f32[1024,16]{0,1:T(8,128)S(1)} %get-tuple-element.11), channel_id=1, source_target_pairs={{0,16},{4,20},{8,24},{12,28},{16,0},{20,4},{24,8},{28,12},{1,17},{... | collective-permute-start | bytes 196616 | tf_op jit(solution)/shard_map/ppermute | solution.py:104
  133.8 31.8 %collective-permute-start = (f32[1024,16]{0,1:T(8,128)S(1)}, f32[1024,16]{0,1:T(8,128)S(1)}, u32[]{:S(2)}, u32[]{:S(2)}) collective-permute-start(f32[1024,16]{0,1:T(8,128)S(1)} %get-tuple-element.14), channel_id=1, source_target_pairs={{0,4},{4,8},{8,12},{12,16},{16,20},{20,24},{24,28},{28,0},{1,5},{5... | collective-permute-start | bytes 196616 | tf_op jit(solution)/shard_map/ppermute | solution.py:104
  165.6 5.2 %collective-permute-start.1 = (f32[1024,16]{0,1:T(8,128)S(1)}, f32[1024,16]{0,1:T(8,128)S(1)}, u32[]{:S(2)}, u32[]{:S(2)}) collective-permute-start(f32[1024,16]{0,1:T(8,128)S(1)} %get-tuple-element.13), channel_id=1, source_target_pairs={{0,8},{4,12},{8,16},{12,20},{16,24},{20,28},{24,0},{28,4},{1,9},{5... | collective-permute-start | bytes 196616 | tf_op jit(solution)/shard_map/ppermute | solution.py:104
  170.8 4.3 %collective-permute-start.2 = (f32[1024,16]{0,1:T(8,128)S(1)}, f32[1024,16]{0,1:T(8,128)S(1)}, u32[]{:S(2)}, u32[]{:S(2)}) collective-permute-start(f32[1024,16]{0,1:T(8,128)S(1)} %get-tuple-element.12), channel_id=1, source_target_pairs={{0,12},{4,16},{8,20},{12,24},{16,28},{20,0},{24,4},{28,8},{1,13},{... | collective-permute-start | bytes 196616 | tf_op jit(solution)/shard_map/ppermute | solution.py:104
  197.7 126.6 %reduce-scatter.7.cloned.1.call-start = ((), (), s32[]{:S(2)}) async-start(), calls=%async_computation.4 | async-start | bytes 811008
Sparse Core Ops, SparseCore 0:
  197.8 19.0 reduce-scatter.4
  230.4 93.7 reduce-scatter.6
